TPU v7x, 128 devices: a whole 4x4x4 slice. The times are simulated.
128 devices in a mesh: req: 16 (over x, y), mlp: 8 (over z, core).
Axes of the slice: x: 4, y: 4, z: 4, core: 2. Of those that a mesh axis runs over, the one named last changes fastest.
Arguments:
- tokens: bfloat16 [4096, 2048], P(('req', 'mlp')), may hold values from -6 to 6
- cached_states: float32 [256, 8, 256, 512], P('req', 'mlp'), may hold values from -12 to 12
- prompt_lengths: int32 [256], P('req'), may hold values from 1 to 4096, as said below
- accepted: int32 [256], P('req'), may hold values from 1 to 16, as said below
- owner_slot: int32 [256], P('req'), may hold values from 0 to 255, as said below
- w_query: bfloat16 [2048, 2048], P(None, 'mlp'), may hold values from -0.125 to 0.125
- w_key: bfloat16 [2048, 2048], P(None, 'mlp'), may hold values from -0.125 to 0.125
- w_value: bfloat16 [2048, 4096], P(None, 'mlp'), may hold values from -0.125 to 0.125
- w_gate_ret: bfloat16 [2048, 4096], P(None, 'mlp'), may hold values from -0.125 to 0.125
- w_out: bfloat16 [4096, 2048], P('mlp'), may hold values from -0.09375 to 0.09375
- w_gate: bfloat16 [2048, 4096], P('req', 'mlp'), may hold values from -0.125 to 0.125
- w_up: bfloat16 [2048, 4096], P('req', 'mlp'), may hold values from -0.125 to 0.125
- w_down: bfloat16 [4096, 2048], P('mlp', 'req'), may hold values from -0.09375 to 0.09375
Outputs:
- mixed: bfloat16 [4096, 2048], P(('req', 'mlp'))
- new_states: float32 [256, 8, 256, 512], P('req', 'mlp')
Inputs may be any that keep to these rules, and one draw needn't show every extreme that they name: `prompt_lengths`: request r belongs to tenant k = (4 r) // 256, so the four tenants hold consecutive ranges of 64 requests; its prompt length is drawn evenly from 1 to 4^(k + 3). `accepted`: number of leading drafts of request r that are kept, drawn evenly for each request. A permutation of the requests; for request r on req block i = r // 16, owner_slot[r] = j * 16 + i + c with owner block j and 0 <= c < 1, and each pair (j, c) occurs exactly once within a block.
All inputs are finite; a program needn't handle non-finite values.
Results may differ from a plain program's by a relative error of at most 0.017.
Values may be sent and summed in bfloat16 or wider, within the bound.
No kernel may reach another device: no remote copies, remote signals or barrier semaphores. Data moves between devices by JAX's collectives and lax.ppermute only.
A program may use at most 128 MiB of HBM per device.

v0:
```python
import math
import jax
import jax.numpy as jnp
from jax import lax
from jax.sharding import PartitionSpec as P

DRAFT = 16
epsilon = 1e-05


def layer_norm(inputs):
    average = jnp.mean(inputs, axis=-1, keepdims=True)
    centred = inputs - average
    variance = jnp.mean(centred * centred, axis=-1, keepdims=True)
    return centred * lax.rsqrt(variance + epsilon)


def decays(head_count, first_head):
    head_index = jnp.arange(head_count, dtype=jnp.float32) + first_head
    return 1.0 - jnp.exp2(-5.0 - head_index)


def rotate(inputs, positions):
    half_width = inputs.shape[-1] // 2
    frequencies = jnp.exp(
        -math.log(10000.0) * jnp.arange(half_width, dtype=jnp.float32) / half_width
    )
    angles = positions[:, :, None] * frequencies[None, None, :]
    cosine_part = jnp.cos(angles)[:, :, None, :]
    sine_part = jnp.sin(angles)[:, :, None, :]
    front_half = inputs[..., :half_width]
    back_half = inputs[..., half_width:]
    return jnp.concatenate(
        [
            front_half * cosine_part - back_half * sine_part,
            front_half * sine_part + back_half * cosine_part,
        ],
        axis=-1,
    )


def state_weights(states, accepted, gammas, draft_count):
    draft_pos = jnp.arange(draft_count, dtype=jnp.float32)
    accepted_f = accepted.astype(jnp.float32)
    exponent = accepted_f[:, None, None] - 1.0 - draft_pos[None, None, :]
    draft_weights = jnp.where(
        exponent >= 0, jnp.power(gammas[None, :, None], jnp.maximum(exponent, 0.0)), 0.0
    )
    old_part = jnp.power(gammas[None, :], accepted_f[:, None])[:, :, None, None] * states
    return (old_part, draft_weights)


def fold_update(key_rows, values, draft_weights):
    scaled = key_rows.astype(jnp.float32) * jnp.transpose(draft_weights, (0, 2, 1))[..., None]
    return jnp.einsum(
        "rshd,rshv->rhdv", scaled, values.astype(jnp.float32), precision=lax.Precision.HIGHEST
    )


def retain_outputs(queries, key_rows, values, states, gammas):
    draft_count = queries.shape[1]
    draft_pos = jnp.arange(draft_count, dtype=jnp.float32)
    distance = draft_pos[:, None] - draft_pos[None, :]
    decay_mask = jnp.where(
        distance[None] >= 0, jnp.power(gammas[:, None, None], jnp.maximum(distance, 0.0)[None]), 0.0
    )
    scores = jnp.einsum("rthd,rshd->rhts", queries, key_rows, preferred_element_type=jnp.float32)
    weights = (scores * decay_mask[None]).astype(jnp.bfloat16)
    within = jnp.einsum("rhts,rshv->rthv", weights, values, preferred_element_type=jnp.float32)
    carried = jnp.einsum(
        "rthd,rhdv->rthv", queries.astype(jnp.float32), states, precision=lax.Precision.HIGHEST
    )
    carried = carried * jnp.power(gammas[None, None, :, None], draft_pos[None, :, None, None] + 1.0)
    return within + carried


def per_device(
    tokens,
    cached_states,
    prompt_lengths,
    accepted,
    owner_slot,
    w_query,
    w_key,
    w_value,
    w_gate_ret,
    w_out,
    w_gate,
    w_up,
    w_down,
):
    requests = cached_states.shape[0]
    heads_here = cached_states.shape[1]
    key_width = cached_states.shape[2]
    value_width = cached_states.shape[3]
    draft_count = DRAFT
    per_peer = requests // lax.axis_size("req")
    first_head = (lax.axis_index("mlp") * heads_here).astype(jnp.float32)
    gammas = decays(heads_here, first_head)
    target_pos = owner_slot // requests * per_peer + owner_slot % per_peer
    local_ids = jnp.arange(requests, dtype=jnp.int32)
    send_order = jnp.sum(
        jnp.where(target_pos[None, :] == local_ids[:, None], local_ids[None, :], 0), axis=1
    )
    old_part, draft_weights = state_weights(cached_states, accepted, gammas, draft_count)
    group_rows = lax.all_gather(tokens, "mlp", axis=0, tiled=True)
    row_count = group_rows.shape[0]
    normed = layer_norm(group_rows.astype(jnp.float32)).astype(jnp.bfloat16)
    queries = jnp.dot(normed, w_query, preferred_element_type=jnp.float32).reshape(
        requests, draft_count, heads_here, key_width
    )
    key_rows = (
        jnp.dot(normed, w_key, preferred_element_type=jnp.float32) * (1.0 / math.sqrt(key_width))
    ).reshape(requests, draft_count, heads_here, key_width)
    values = (
        jnp.dot(normed, w_value, preferred_element_type=jnp.float32)
        .astype(jnp.bfloat16)
        .reshape(requests, draft_count, heads_here, value_width)
    )
    gate_ret = jnp.dot(normed, w_gate_ret, preferred_element_type=jnp.float32).reshape(
        requests, draft_count, heads_here, value_width
    )
    positions = (
        prompt_lengths[:, None] + jnp.arange(draft_count, dtype=jnp.int32)[None, :]
    ).astype(jnp.float32)
    rotated_q = rotate(queries, positions).astype(jnp.bfloat16)
    rotated_k = rotate(key_rows, positions).astype(jnp.bfloat16)
    fresh = old_part + fold_update(rotated_k, values, draft_weights)
    new_states = lax.all_to_all(
        jnp.take(fresh, send_order, axis=0).astype(jnp.bfloat16),
        "req",
        split_axis=0,
        concat_axis=0,
        tiled=True,
    ).astype(jnp.float32)
    outputs = retain_outputs(rotated_q, rotated_k, values, cached_states, gammas)
    joined = (
        (layer_norm(outputs) * jax.nn.silu(gate_ret))
        .astype(jnp.bfloat16)
        .reshape(row_count, heads_here * value_width)
    )
    partials = jnp.dot(joined, w_out, preferred_element_type=jnp.float32)
    share = tokens.shape[0]
    summed = lax.psum(partials.astype(jnp.bfloat16), "mlp").astype(jnp.float32)
    residual = group_rows.astype(jnp.float32) + summed
    hidden_in = layer_norm(residual).astype(jnp.bfloat16)
    residual_share = lax.dynamic_slice_in_dim(residual, lax.axis_index("mlp") * share, share, 0)
    gate_sum = jnp.dot(
        hidden_in,
        lax.all_gather(w_gate, "req", axis=0, tiled=True),
        preferred_element_type=jnp.float32,
    )
    up_sum = jnp.dot(
        hidden_in,
        lax.all_gather(w_up, "req", axis=0, tiled=True),
        preferred_element_type=jnp.float32,
    )
    hidden = (jax.nn.silu(gate_sum) * up_sum).astype(jnp.bfloat16)
    down_terms = jnp.dot(
        hidden,
        lax.all_gather(w_down, "req", axis=1, tiled=True),
        preferred_element_type=jnp.float32,
    )
    mixed = (
        residual_share
        + lax.psum_scatter(
            down_terms.astype(jnp.bfloat16), "mlp", scatter_dimension=0, tiled=True
        ).astype(jnp.float32)
    ).astype(jnp.bfloat16)
    return (mixed, new_states)


def solution(mesh):
    return jax.shard_map(
        per_device,
        mesh=mesh,
        in_specs=(
            P(("req", "mlp"), None),
            P("req", "mlp", None, None),
            P("req"),
            P("req"),
            P("req"),
            P(None, "mlp"),
            P(None, "mlp"),
            P(None, "mlp"),
            P(None, "mlp"),
            P("mlp", None),
            P("req", "mlp"),
            P("req", "mlp"),
            P("mlp", "req"),
        ),
        out_specs=(P(("req", "mlp"), None), P("req", "mlp", None, None)),
        check_vma=False,
    )
```

profile of v0, /device:TPU:0, one launch (start us, length us, event | category | flops | bytes accessed | tf_op | source)
XLA Modules:
  0.0 292.6 jit_solution(9923239641830720972)
XLA Ops:
  8.0 0.0 copy-start
  8.0 0.0 copy-start.13
  8.0 0.0 all-gather.5.cloned.1.call-start
  8.1 0.7 all-gather.5.cloned.1.call-update
  8.8 0.0 all-reduce.2.cloned.1.call-start
  8.9 1.3 convert_add_fusion.1
  10.2 0.7 add_convert_fusion.1
  10.9 0.7 power_select_fusion
  11.6 25.0 %all-gather.5.cloned.1.call-done = bf16[256,2048]{1,0:T(8,128)(2,1)} async-done(((bf16[32,2048]{1,0:T(8,128)(2,1)}), bf16[256,2048]{1,0:T(8,128)(2,1)}) %all-gather.5.cloned.1.call-update) | async-done | bytes 1048592 | tf_op jit(solution)/shard_map/all_gather | solution.py:106
  36.6 1.6 convert_reduce_fusion
  38.3 0.0 copy-start.8
  38.3 2.0 fusion.7
  40.2 0.0 copy-done.13
  40.2 0.0 copy-start.10
  40.3 1.7 fusion.62
  42.0 2.0 convolution_multiply_fusion.1
  44.0 0.6 fusion.46
  44.6 0.0 copy-start.5
  44.6 0.0 copy-start.6
  44.7 0.6 copy-done.5
  45.3 0.0 copy-done.6
  45.3 0.0 copy-done.1
  45.3 3.7 %fusion.14 = f32[16,1,512,16]{2,3,0,1:T(8,128)} fusion(f32[16,1,256,512]{3,2,1,0:T(8,128)S(1)} %copy-done.1, f32[16]{0:T(128)S(1)} %add_power_fusion, bf16[16,16,128]{2,1,0:T(8,128)(2,1)S(1)} %get-tuple-element.10, bf16[16,16,128]{2,1,0:T(8,128)(2,1)S(1)} %get-tuple-element.11), kind=kOutput, calls=%fused_computation.25 | convolution fusion | flops 403046400 | bytes 9044032 | tf_op jit(solution)/shard_map/rthd,rhdv->rthv/dot_general | solution.py:70
  49.0 0.0 copy-done.8
  49.0 0.0 copy-done.10
  49.0 0.0 copy-done.2
  49.0 0.8 convolution_convert_fusion.2
  49.7 2.2 fusion.65
  52.0 1.2 multiply_reduce_fusion.1
  53.2 0.0 copy-start.3
  53.2 2.4 fusion.59
  55.7 0.0 copy-done.3
  55.7 0.2 multiply_convert_fusion.1
  55.9 0.0 copy-start.14
  56.0 1.7 convolution_convert_fusion.1
  57.7 0.0 all-reduce.2.cloned.1.call-update
  57.7 0.0 all-gather.7.cloned.1.call-start
  57.7 0.5 all-gather.7.cloned.1.call-update
  58.3 0.0 all-gather.9.cloned.1.call-start
  58.3 0.5 all-gather.9.cloned.1.call-update
  58.9 0.0 all-gather.11.cloned.1.call-start
  58.9 0.5 all-gather.11.cloned.1.call-update
  59.5 0.1 select_reduce_fusion
  59.6 0.5 compare_and_fusion
  60.1 0.0 copy-done.7
  60.1 8.5 %fusion.1 = bf16[16,256,512]{2,1,0:T(8,128)(2,1)} fusion(f32[16,1,256,512]{3,2,1,0:T(8,128)} %param.14, f32[16]{0:T(128)S(1)} %copy-done.9, bf16[16,16,512]{2,1,0:T(8,128)(2,1)S(1)} %bitcast.68, f32[16,16]{1,0:T(8,128)S(1)} %copy-done.7, bf16[16,16,128]{2,1,0:T(8,128)(2,1)S(1)} %get-tuple-element.7, bf16[16,16,128]{2,1,0:T(8,128)(2,1)S(1)} %get-tuple-element.6), kind=kOutput, calls=%fused_computation.4 | convolution fusion | flops 409272320 | bytes 12977216 | tf_op jit(solution)/shard_map/rshd,rshv->rhdv/dot_general | solution.py:55
  68.7 5.1 %gather_fusion = bf16[16,256,512]{2,1,0:T(8,128)(2,1)} fusion(bf16[16,256,512]{2,1,0:T(8,128)(2,1)} %fusion.1, s32[1024]{0:T(1024)S(1)} %pad_clamp_fusion), kind=kCustom, calls=%fused_computation | custom fusion | bytes 8388672 | tf_op jit(solution)/shard_map/jit(_take)/gather | solution.py:130
  73.7 5.5 %fusion.4 = bf16[16,1,256,512]{3,2,1,0:T(8,128)(2,1)} fusion(bf16[16,256,512]{2,1,0:T(8,128)(2,1)} %gather_fusion, pred[16]{0:T(512)(128)(4,1)S(1)} %copy-done.11), kind=kLoop, calls=%fused_computation.8 | loop fusion | flops 2097152 | bytes 8388624 | tf_op jit(solution)/shard_map/convert_element_type | solution.py:130
  79.2 6.9 %all-to-all-start = ((bf16[16,1,256,512]{3,2,1,0:T(8,128)(2,1)}), bf16[16,1,256,512]{3,2,1,0:T(8,128)(2,1)}, u32[]{:S(2)}, u32[]{:S(2)}) async-start(bf16[16,1,256,512]{3,2,1,0:T(8,128)(2,1)} %fusion.4), calls=%async_computation.1 | async-start | bytes 8388608 | tf_op jit(solution)/shard_map/all_to_all | solution.py:129
  86.1 0.2 reduce-scatter.2.cloned.1.call-start
  86.3 35.1 %all-reduce.2.cloned.1.call-done = bf16[256,2048]{1,0:T(8,128)(2,1)} async-done(((bf16[256,2048]{1,0:T(8,128)(2,1)}), bf16[256,2048]{1,0:T(8,128)(2,1)}) %all-reduce.2.cloned.1.call-update) | async-done | bytes 1048592 | tf_op jit(solution)/shard_map/psum | solution.py:144
  121.4 2.9 convert_add_fusion
  124.3 0.0 copy-done.4
  124.3 0.5 multiply_reduce_fusion
  124.8 18.6 %all-gather.7.cloned.1.call-done = bf16[2048,512]{1,0:T(8,128)(2,1)} async-done(((bf16[128,512]{1,0:T(8,128)(2,1)}), bf16[2048,512]{1,0:T(8,128)(2,1)}) %all-gather.7.cloned.1.call-update) | async-done | bytes 2097168 | tf_op jit(solution)/shard_map/all_gather | solution.py:150
  143.5 3.5 %fusion.58 = f32[256,512]{1,0:T(8,128)} fusion(bf16[2048,512]{1,0:T(8,128)(2,1)} %all-gather.7.cloned.1.call-done, f32[256]{0:T(256)S(1)} %add_rsqrt_fusion.1, f32[256]{0:T(256)S(1)} %broadcast_multiply_fusion.1, bf16[256,2048]{1,0:T(8,128)(2,1)} %all-reduce.2.cloned.1.call-done, bf16[256,2048]{1,0:T(8,128)(2,1)S(1)} %copy-done.2), kind=kOutput, calls=%fused_computation.101 | convolution fusion | flops 540016640 | bytes 4720640 | tf_op jit(solution)/shard_map/dot_general | solution.py:148
  147.0 51.2 %all-gather.9.cloned.1.call-done = bf16[2048,512]{1,0:T(8,128)(2,1)} async-done(((bf16[128,512]{1,0:T(8,128)(2,1)}), bf16[2048,512]{1,0:T(8,128)(2,1)}) %all-gather.9.cloned.1.call-update) | async-done | bytes 2097168 | tf_op jit(solution)/shard_map/all_gather | solution.py:155
  198.2 48.6 %all-gather.11.cloned.1.call-done = bf16[512,2048]{1,0:T(8,128)(2,1)} async-done(((bf16[512,128]{1,0:T(8,128)(2,1)}), bf16[512,2048]{1,0:T(8,128)(2,1)}) %all-gather.11.cloned.1.call-update) | async-done | bytes 2097168 | tf_op jit(solution)/shard_map/all_gather | solution.py:161
  246.8 5.2 %convolution_convert_fusion = bf16[256,2048]{1,0:T(8,128)(2,1)} fusion(bf16[512,2048]{1,0:T(8,128)(2,1)} %all-gather.11.cloned.1.call-done, bf16[2048,512]{1,0:T(8,128)(2,1)} %all-gather.9.cloned.1.call-done, f32[256,512]{1,0:T(8,128)} %fusion.58, f32[256]{0:T(256)S(1)} %add_rsqrt_fusion.1, f32[256]{0:T(256)S(1)} %broadcast_multiply_fusion.1, ...), kind=kOutput, calls=%fused_computation.12 | convolution fusion | flops 1078198272 | bytes 7866368 | tf_op jit(solution)/shard_map/dot_general | solution.py:159
  252.0 0.0 reduce-scatter.2.cloned.1.call-update
  252.0 0.0 all-to-all-done
  252.0 6.7 %convert_element_type.101 = f32[16,1,256,512]{3,2,1,0:T(8,128)} convert(bf16[16,1,256,512]{3,2,1,0:T(8,128)(2,1)} %all-to-all-done) | non-fusion elementwise | flops 2097152 | bytes 12582912 | tf_op jit(solution)/shard_map/convert_element_type | solution.py:135
  258.7 24.9 %reduce-scatter.2.cloned.1.call-done = bf16[32,2048]{1,0:T(8,128)(2,1)} async-done(((bf16[256,2048]{1,0:T(8,128)(2,1)}), bf16[32,2048]{1,0:T(8,128)(2,1)}) %reduce-scatter.2.cloned.1.call-update) | async-done | bytes 131088 | tf_op jit(solution)/shard_map/reduce_scatter | solution.py:166
  283.6 1.7 add_convert_fusion
  (23 shorter events, 0.1 us)
Async XLA Ops:
  8.0 47.9 %copy-start = (bf16[512,2048]{1,0:T(8,128)(2,1)S(1)}, bf16[512,2048]{1,0:T(8,128)(2,1)}, u32[]{:S(2)}) copy-start(bf16[512,2048]{1,0:T(8,128)(2,1)} %param.22) | copy-start | bytes 6291460
  8.0 32.2 %copy-start.13 = (bf16[2048,256]{1,0:T(8,128)(2,1)S(1)}, bf16[2048,256]{1,0:T(8,128)(2,1)}, u32[]{:S(2)}) copy-start(bf16[2048,256]{1,0:T(8,128)(2,1)} %param.18) | copy-start | bytes 3145732
  8.0 28.6 %all-gather.5.cloned.1.call-start = ((), (), s32[]{:S(2)}) async-start(), calls=%async_computation.2 | async-start | bytes 1179648 | tf_op jit(solution)/shard_map/all_gather | solution.py:106
  8.8 112.6 %all-reduce.2.cloned.1.call-start = ((), (), s32[]{:S(2)}) async-start(), calls=%async_computation.3 | async-start | bytes 2097152 | tf_op jit(solution)/shard_map/psum | solution.py:144
  36.6 8.6 %copy-start.1 = (f32[16,1,256,512]{3,2,1,0:T(8,128)S(1)}, f32[16,1,256,512]{3,2,1,0:T(8,128)}, u32[]{:S(2)}) copy-start(f32[16,1,256,512]{3,2,1,0:T(8,128)} %param.14) | copy-start | bytes 25165828
  38.3 10.7 %copy-start.8 = (f32[256]{0:T(256)}, f32[256]{0:T(256)S(1)}, u32[]{:S(2)}) copy-start(f32[256]{0:T(256)S(1)} %broadcast_multiply_fusion.2) | copy-start | bytes 3076
  40.2 8.7 %copy-start.10 = (f32[256]{0:T(256)}, f32[256]{0:T(256)S(1)}, u32[]{:S(2)}) copy-start(f32[256]{0:T(256)S(1)} %add_rsqrt_fusion.2) | copy-start | bytes 3076
  44.6 0.6 copy-start.5
  44.6 0.6 copy-start.6
  45.3 3.7 %copy-start.2 = (bf16[256,2048]{1,0:T(8,128)(2,1)S(1)}, bf16[256,2048]{1,0:T(8,128)(2,1)}, u32[]{:S(2)}) copy-start(bf16[256,2048]{1,0:T(8,128)(2,1)} %all-gather.5.cloned.1.call-done) | copy-start | bytes 3145732
  45.3 3.7 %copy-start.12 = (bf16[2048,512]{1,0:T(8,128)(2,1)S(1)}, bf16[2048,512]{1,0:T(8,128)(2,1)}, u32[]{:S(2)}) copy-start(bf16[2048,512]{1,0:T(8,128)(2,1)} %param.20) | copy-start | bytes 6291460
  53.2 2.4 copy-start.3
  55.9 3.5 %copy-start.14 = (s32[16]{0:T(128)S(1)}, s32[16]{0:T(128)}, u32[]{:S(2)}) copy-start(s32[16]{0:T(128)} %param.17) | copy-start | bytes 196
  55.9 4.2 %copy-start.7 = (f32[16,16]{1,0:T(8,128)S(1)}, f32[16,16]{1,0:T(8,128)}, u32[]{:S(2)}) copy-start(f32[16,16]{1,0:T(8,128)} %get-tuple-element.16) | copy-start | bytes 3076
  55.9 4.2 %copy-start.9 = (f32[16]{0:T(128)S(1)}, f32[16]{0:T(128)}, u32[]{:S(2)}) copy-start(f32[16]{0:T(128)} %get-tuple-element.13) | copy-start | bytes 196
  57.7 85.8 %all-gather.7.cloned.1.call-start = ((), (), s32[]{:S(2)}) async-start(), calls=%async_computation.4 | async-start | bytes 2228224 | tf_op jit(solution)/shard_map/all_gather | solution.py:150
  58.3 139.9 %all-gather.9.cloned.1.call-start = ((), (), s32[]{:S(2)}) async-start(), calls=%async_computation.5 | async-start | bytes 2228224 | tf_op jit(solution)/shard_map/all_gather | solution.py:155
  58.9 187.9 %all-gather.11.cloned.1.call-start = ((), (), s32[]{:S(2)}) async-start(), calls=%async_computation.6 | async-start | bytes 2228224 | tf_op jit(solution)/shard_map/all_gather | solution.py:161
  68.7 5.1 %copy-start.11 = (pred[16]{0:T(512)(128)(4,1)S(1)}, pred[16]{0:T(512)(128)(4,1)}, u32[]{:S(2)}) copy-start(pred[16]{0:T(512)(128)(4,1)} %compare_and_fusion) | copy-start | bytes 52
  79.2 172.8 %all-to-all-start = ((bf16[16,1,256,512]{3,2,1,0:T(8,128)(2,1)}), bf16[16,1,256,512]{3,2,1,0:T(8,128)(2,1)}, u32[]{:S(2)}, u32[]{:S(2)}) async-start(bf16[16,1,256,512]{3,2,1,0:T(8,128)(2,1)} %fusion.4), calls=%async_computation.1 | async-start | bytes 8388608 | tf_op jit(solution)/shard_map/all_to_all | solution.py:129
  86.1 197.5 %reduce-scatter.2.cloned.1.call-start = ((), (), s32[]{:S(2)}) async-start(), calls=%async_computation.7 | async-start | bytes 1179648 | tf_op jit(solution)/shard_map/reduce_scatter | solution.py:166
  121.4 2.9 copy-start.4
Sparse Core Ops, SparseCore 0:
  10.6 26.0 all-gather.4
  57.8 63.5 all-reduce.1
  252.1 31.4 reduce-scatter.1
Sparse Core Ops, SparseCore 1:
  60.3 83.1 all-gather.6
  145.5 52.7 all-gather.8
  200.2 46.5 all-gather.10
where the time goes:
time: 293 us
  waiting for transfers between devices  206 us (70%)
  matrix products  31.8 us (11%)
  other arithmetic  26.4 us (9%)
  between operations  15.7 us (5%)
  starting transfers between devices  7.29 us (2%)
  local copies, waits for them, and re-layouts  5.76 us (2%)
    all_gather x1, waiting for transfers between devices, per_device(): lax.all_gather(w_up, 'req', axis=0, tiled=True)  51.2 us
    all_gather x1, waiting for transfers between devices, per_device(): lax.all_gather(w_down, 'req', axis=1, tiled=True)  48.6 us
    psum x1, waiting for transfers between devices, per_device(): summed = lax.psum(partials.astype(jnp.bfloat16), 'mlp').astype(jnp.float32)  35.1 us
    all_gather x1, waiting for transfers between devices, per_device(): group_rows = lax.all_gather(tokens, 'mlp', axis=0, tiled=True)  25 us
    reduce_scatter x1, waiting for transfers between devices, per_device(): lax.psum_scatter(down_terms.astype(jnp.bfloat16), 'mlp', scatter_dimensio...  24.9 us
    all_gather x1, waiting for transfers between devices, per_device(): lax.all_gather(w_gate, 'req', axis=0, tiled=True)  18.6 us
    dot_general x1, matrix products, fold_update(): jnp.einsum('rshd,rshv->rhdv', scaled, values.astype(jnp.float32), precisi...  8.54 us
    all_to_all x1, starting transfers between devices, per_device(): lax.all_to_all(jnp.take(fresh, send_order, axis=0).astype(jnp.bfloat16),...  6.87 us
  transfers between devices with their start and end apart: 7, of which 6 were waited for; matrix products, arithmetic and copies ran while one was open for 14% of the time, Pallas kernels for 0%

commit v1 on v0

--- a/solution.py
+++ b/solution.py
@@ -156,11 +156,42 @@
         preferred_element_type=jnp.float32,
     )
     hidden = (jax.nn.silu(gate_sum) * up_sum).astype(jnp.bfloat16)
-    down_terms = jnp.dot(
-        hidden,
-        lax.all_gather(w_down, "req", axis=1, tiled=True),
-        preferred_element_type=jnp.float32,
-    )
+
+    def _fix_numbers(message):
+        newest = lax.axis_size("req")
+        outer, odd, kept_arr = (newest, lax.axis_index("req"), message.shape[1])
+        windows = []
+        for dev_j, t in enumerate(message.shape):
+            windows.append(t * outer if dev_j == 1 else t)
+        low = lax.dynamic_update_slice_in_dim(
+            jnp.zeros(windows, message.dtype), message, odd * kept_arr, axis=1
+        )
+        state_next = raw_out = message
+        u = 1
+        while u < outer // 2 + 1:
+            made = []
+            dev_j = 0
+            while dev_j < outer:
+                made.append((dev_j, (dev_j + 1) % outer))
+                dev_j += 1
+            state_next = lax.ppermute(state_next, "req", made)
+            low = lax.dynamic_update_slice_in_dim(
+                low, state_next, (odd - u) % outer * kept_arr, axis=1
+            )
+            if 2 * u < outer:
+                buffer = []
+                dev_j = 0
+                while dev_j < outer:
+                    buffer.append((dev_j, (dev_j - 1) % outer))
+                    dev_j += 1
+                raw_out = lax.ppermute(raw_out, "req", buffer)
+                low = lax.dynamic_update_slice_in_dim(
+                    low, raw_out, (odd + u) % outer * kept_arr, axis=1
+                )
+            u = u + 1
+        return low
+
+    down_terms = jnp.dot(hidden, _fix_numbers(w_down), preferred_element_type=jnp.float32)
     mixed = (
         residual_share
         + lax.psum_scatter(

time: 293 us -> 237 us (0.81)
  waiting for transfers between devices: 206 us -> 99.6 us
  starting transfers between devices: 7.29 us -> 43.7 us
  local copies, waits for them, and re-layouts: 5.76 us -> 19.3 us
    all_gather x1 -> x0, waiting for transfers between devices: 48.6 us -> none  [per_device(): lax.all_gather(w_down, 'req', axis=1, tiled=True)]
    ppermute x0 -> x15, starting transfers between devices: none -> 38.9 us  [the longest x7 37.3 us: _fix_numbers(): raw_out = lax.ppermute(raw_out, 'req', buffer)]
    psum x1, waiting for transfers between devices: 35.1 us -> 0.02 us  [per_device(): summed = lax.psum(partials.astype(jnp.bfloat16), 'mlp').astype(jnp.float32)]
    all_gather x1, waiting for transfers between devices: 51.2 us -> 16.8 us  [per_device(): lax.all_gather(w_up, 'req', axis=0, tiled=True)]
    ppermute x0 -> x15, waiting for transfers between devices: none -> 20.6 us  [the longest x8 11.9 us: _fix_numbers(): state_next = lax.ppermute(state_next, 'req', made)]
    all_gather x1, waiting for transfers between devices: 18.6 us -> 0.02 us  [per_device(): lax.all_gather(w_gate, 'req', axis=0, tiled=True)]
    all_to_all x1, waiting for transfers between devices: 0.01 us -> 17.8 us  [per_device(): lax.all_to_all(jnp.take(fresh, send_order, axis=0).astype(jnp.bfloat16),...]
    dynamic_update_slice x0 -> x16, local copies, waits for them, and re-layouts: none -> 12.7 us  [the longest x8 6.33 us: _fix_numbers(): lax.dynamic_update_slice_in_dim(low, state_next, (odd - u) % outer * kept...]
  transfers between devices with their start and end apart: 7 -> 21, of which waited for: 6 -> 14; matrix products, arithmetic and copies ran while one was open for 14% -> 23% of each run, Pallas kernels for 0% -> 0%
where the time goes in v1:
time: 237 us
  waiting for transfers between devices  99.6 us (42%)
  starting transfers between devices  43.7 us (18%)
  matrix products  32.1 us (14%)
  other arithmetic  26 us (11%)
  local copies, waits for them, and re-layouts  19.3 us (8%)
  between operations  15.9 us (7%)
    ppermute x7, starting transfers between devices, _fix_numbers(): raw_out = lax.ppermute(raw_out, 'req', buffer)  37.3 us
    all_gather x1, waiting for transfers between devices, per_device(): group_rows = lax.all_gather(tokens, 'mlp', axis=0, tiled=True)  25.1 us
    reduce_scatter x1, waiting for transfers between devices, per_device(): lax.psum_scatter(down_terms.astype(jnp.bfloat16), 'mlp', scatter_dimensio...  17.9 us
    all_to_all x1, waiting for transfers between devices, per_device(): lax.all_to_all(jnp.take(fresh, send_order, axis=0).astype(jnp.bfloat16),...  17.8 us
    all_gather x1, waiting for transfers between devices, per_device(): lax.all_gather(w_up, 'req', axis=0, tiled=True)  16.8 us
    ppermute x8, waiting for transfers between devices, _fix_numbers(): state_next = lax.ppermute(state_next, 'req', made)  11.9 us
    ppermute x7, waiting for transfers between devices, _fix_numbers(): raw_out = lax.ppermute(raw_out, 'req', buffer)  8.65 us
    dot_general x1, matrix products, fold_update(): jnp.einsum('rshd,rshv->rhdv', scaled, values.astype(jnp.float32), precisi...  8.54 us
  transfers between devices with their start and end apart: 21, of which 14 were waited for; matrix products, arithmetic and copies ran while one was open for 23% of the time, Pallas kernels for 0%

profile of v1, /device:TPU:0, one launch (start us, length us, event | category | flops | bytes accessed | tf_op | source)
XLA Modules:
  0.0 236.5 jit_solution(13421337423239378367)
XLA Ops:
  8.1 0.7 all-gather.4.cloned.1.call-update
  8.9 1.2 convert_add_fusion.1
  10.1 0.7 add_convert_fusion.1
  10.8 0.7 power_select_fusion
  11.5 25.1 %all-gather.4.cloned.1.call-done = bf16[256,2048]{1,0:T(8,128)(2,1)} async-done(((bf16[32,2048]{1,0:T(8,128)(2,1)}), bf16[256,2048]{1,0:T(8,128)(2,1)}) %all-gather.4.cloned.1.call-update) | async-done | bytes 1048592 | tf_op jit(solution)/shard_map/all_gather | solution.py:106
  36.6 1.6 convert_reduce_fusion
  38.3 2.0 fusion.7
  40.2 2.0 fusion.62
  42.3 2.0 convolution_multiply_fusion.1
  44.3 0.6 fusion.46
  45.0 3.7 %fusion.14 = f32[16,1,512,16]{2,3,0,1:T(8,128)} fusion(f32[16,1,256,512]{3,2,1,0:T(8,128)S(1)} %copy-done.1, f32[16]{0:T(128)S(1)} %add_power_fusion, bf16[16,16,128]{2,1,0:T(8,128)(2,1)S(1)} %get-tuple-element.10, bf16[16,16,128]{2,1,0:T(8,128)(2,1)S(1)} %get-tuple-element.11), kind=kOutput, calls=%fused_computation.25 | convolution fusion | flops 403046400 | bytes 9044032 | tf_op jit(solution)/shard_map/rthd,rhdv->rthv/dot_general | solution.py:70
  48.7 0.8 convolution_convert_fusion.2
  49.4 2.2 fusion.65
  51.7 1.2 multiply_reduce_fusion.1
  53.0 2.4 %fusion.59 = f32[256,512]{1,0:T(8,128)S(1)} fusion(bf16[2048,512]{1,0:T(8,128)(2,1)} %param.21, bf16[256,2048]{1,0:T(8,128)(2,1)S(1)} %copy-done.2, f32[256]{0:T(256)} %copy-done.11, f32[256]{0:T(256)} %copy-done.9), kind=kOutput, calls=%fused_computation.118 | convolution fusion | flops 538968064 | bytes 3672064 | tf_op jit(solution)/shard_map/dot_general | solution.py:120
  55.4 0.2 multiply_convert_fusion.1
  55.6 1.8 convolution_convert_fusion.1
  57.5 0.5 all-gather.6.cloned.1.call-update
  58.1 1.6 collective-permute-start
  59.6 3.9 %collective-permute-start.1 = (bf16[512,128]{1,0:T(8,128)(2,1)}, bf16[512,128]{1,0:T(8,128)(2,1)}, u32[]{:S(2)}, u32[]{:S(2)}) collective-permute-start(bf16[512,128]{1,0:T(8,128)(2,1)} %param.25), channel_id=1, source_target_pairs={{0,120},{8,0},{16,8},{24,16},{32,24},{40,32},{48,40},{56,48},{64,5... | collective-permute-start | bytes 393224 | tf_op jit(solution)/shard_map/ppermute | solution.py:187
  64.0 1.6 broadcast_in_dim.22
  65.6 0.7 constant_dynamic-update-slice_fusion.15
  66.3 1.1 collective-permute-done
  67.5 5.3 %collective-permute-start.3 = (bf16[512,128]{1,0:T(8,128)(2,1)}, bf16[512,128]{1,0:T(8,128)(2,1)S(1)}, u32[]{:S(2)}, u32[]{:S(2)}) collective-permute-start(bf16[512,128]{1,0:T(8,128)(2,1)} %collective-permute-done.1), channel_id=1, source_target_pairs={{0,120},{8,0},{16,8},{24,16},{32,24},{40,32},{48,40},{56,48},{64,5... | collective-permute-start | bytes 393224 | tf_op jit(solution)/shard_map/ppermute | solution.py:187
  72.8 1.6 constant_dynamic-update-slice_fusion.14
  74.4 1.6 constant_dynamic-update-slice_fusion.13
  76.1 5.4 %collective-permute-start.5 = (bf16[512,128]{1,0:T(8,128)(2,1)S(1)}, bf16[512,128]{1,0:T(8,128)(2,1)S(1)}, u32[]{:S(2)}, u32[]{:S(2)}) collective-permute-start(bf16[512,128]{1,0:T(8,128)(2,1)S(1)} %collective-permute-done.3), channel_id=1, source_target_pairs={{0,120},{8,0},{16,8},{24,16},{32,24},{40,32},{48,40},{56,48},{64,5... | collective-permute-start | bytes 393224 | tf_op jit(solution)/shard_map/ppermute | solution.py:187
  81.5 0.7 constant_dynamic-update-slice_fusion.12
  82.2 0.7 constant_dynamic-update-slice_fusion.11
  82.8 1.9 collective-permute-done.4
  84.8 5.3 %collective-permute-start.7 = (bf16[512,128]{1,0:T(8,128)(2,1)S(1)}, bf16[512,128]{1,0:T(8,128)(2,1)S(1)}, u32[]{:S(2)}, u32[]{:S(2)}) collective-permute-start(bf16[512,128]{1,0:T(8,128)(2,1)S(1)} %collective-permute-done.5), channel_id=1, source_target_pairs={{0,120},{8,0},{16,8},{24,16},{32,24},{40,32},{48,40},{56,48},{64,5... | collective-permute-start | bytes 393224 | tf_op jit(solution)/shard_map/ppermute | solution.py:187
  90.1 0.7 constant_dynamic-update-slice_fusion.10
  90.8 0.7 constant_dynamic-update-slice_fusion.9
  91.5 1.6 collective-permute-done.6
  93.1 2.0 collective-permute-done.7
  95.1 5.8 %collective-permute-start.9 = (bf16[512,128]{1,0:T(8,128)(2,1)S(1)}, bf16[512,128]{1,0:T(8,128)(2,1)S(1)}, u32[]{:S(2)}, u32[]{:S(2)}) collective-permute-start(bf16[512,128]{1,0:T(8,128)(2,1)S(1)} %collective-permute-done.7), channel_id=1, source_target_pairs={{0,120},{8,0},{16,8},{24,16},{32,24},{40,32},{48,40},{56,48},{64,5... | collective-permute-start | bytes 393224 | tf_op jit(solution)/shard_map/ppermute | solution.py:187
  100.9 0.7 constant_dynamic-update-slice_fusion.8
  101.6 0.7 constant_dynamic-update-slice_fusion.7
  102.4 4.0 %collective-permute-done.9 = bf16[512,128]{1,0:T(8,128)(2,1)S(1)} collective-permute-done((bf16[512,128]{1,0:T(8,128)(2,1)S(1)}, bf16[512,128]{1,0:T(8,128)(2,1)S(1)}, u32[]{:S(2)}, u32[]{:S(2)}) %collective-permute-start.9) | collective-permute-done | bytes 131104 | tf_op jit(solution)/shard_map/ppermute | solution.py:187
  106.5 5.8 %collective-permute-start.11 = (bf16[512,128]{1,0:T(8,128)(2,1)S(1)}, bf16[512,128]{1,0:T(8,128)(2,1)S(1)}, u32[]{:S(2)}, u32[]{:S(2)}) collective-permute-start(bf16[512,128]{1,0:T(8,128)(2,1)S(1)} %collective-permute-done.9), channel_id=1, source_target_pairs={{0,120},{8,0},{16,8},{24,16},{32,24},{40,32},{48,40},{56,48},{64,5... | collective-permute-start | bytes 393224 | tf_op jit(solution)/shard_map/ppermute | solution.py:187
  112.3 0.7 constant_dynamic-update-slice_fusion.6
  113.0 0.7 constant_dynamic-update-slice_fusion.5
  113.7 2.1 collective-permute-done.11
  115.8 5.8 %collective-permute-start.13 = (bf16[512,128]{1,0:T(8,128)(2,1)S(1)}, bf16[512,128]{1,0:T(8,128)(2,1)S(1)}, u32[]{:S(2)}, u32[]{:S(2)}) collective-permute-start(bf16[512,128]{1,0:T(8,128)(2,1)S(1)} %collective-permute-done.11), channel_id=1, source_target_pairs={{0,120},{8,0},{16,8},{24,16},{32,24},{40,32},{48,40},{56,48},{64,5... | collective-permute-start | bytes 393224 | tf_op jit(solution)/shard_map/ppermute | solution.py:187
  121.6 0.7 constant_dynamic-update-slice_fusion.4
  122.2 0.7 constant_dynamic-update-slice_fusion.3
  122.9 0.7 constant_dynamic-update-slice_fusion.2
  123.6 0.5 collective-permute-done.13
  124.1 0.7 constant_dynamic-update-slice_fusion.1
  124.8 6.9 %collective-permute-done.14 = bf16[512,128]{1,0:T(8,128)(2,1)S(1)} collective-permute-done((bf16[512,128]{1,0:T(8,128)(2,1)S(1)}, bf16[512,128]{1,0:T(8,128)(2,1)S(1)}, u32[]{:S(2)}, u32[]{:S(2)}) %collective-permute-start.14) | collective-permute-done | bytes 131104 | tf_op jit(solution)/shard_map/ppermute | solution.py:177
  131.7 0.7 constant_dynamic-update-slice_fusion
  132.4 8.5 %fusion.1 = bf16[16,256,512]{2,1,0:T(8,128)(2,1)} fusion(f32[16,1,256,512]{3,2,1,0:T(8,128)} %param.14, f32[16]{0:T(128)S(1)} %copy-done.10, bf16[16,16,512]{2,1,0:T(8,128)(2,1)S(1)} %bitcast.68, f32[16,16]{1,0:T(8,128)S(1)} %copy-done.8, bf16[16,16,128]{2,1,0:T(8,128)(2,1)S(1)} %get-tuple-element.7, bf16[16,16,128]{2,1,0:T(8,128)(2,1)S(1)} %get-tuple-element.6), kind=kOutput, calls=%fused_computation.4 | convolution fusion | flops 409272320 | bytes 12977216 | tf_op jit(solution)/shard_map/rshd,rshv->rhdv/dot_general | solution.py:55
  140.9 4.9 %gather_fusion = bf16[16,256,512]{2,1,0:T(8,128)(2,1)} fusion(bf16[16,256,512]{2,1,0:T(8,128)(2,1)} %fusion.1, s32[1024]{0:T(1024)S(1)} %pad_clamp_fusion), kind=kCustom, calls=%fused_computation | custom fusion | bytes 8388672 | tf_op jit(solution)/shard_map/jit(_take)/gather | solution.py:130
  145.9 5.6 %fusion.4 = bf16[16,1,256,512]{3,2,1,0:T(8,128)(2,1)} fusion(bf16[16,256,512]{2,1,0:T(8,128)(2,1)} %gather_fusion, pred[16]{0:T(512)(128)(4,1)S(1)} %compare_and_fusion), kind=kLoop, calls=%fused_computation.8 | loop fusion | flops 2097152 | bytes 8388624 | tf_op jit(solution)/shard_map/convert_element_type | solution.py:130
  151.4 4.6 %all-to-all-start = ((bf16[16,1,256,512]{3,2,1,0:T(8,128)(2,1)}), bf16[16,1,256,512]{3,2,1,0:T(8,128)(2,1)}, u32[]{:S(2)}, u32[]{:S(2)}) async-start(bf16[16,1,256,512]{3,2,1,0:T(8,128)(2,1)} %fusion.4), calls=%async_computation.1 | async-start | bytes 8388608 | tf_op jit(solution)/shard_map/all_to_all | solution.py:129
  156.1 3.0 %convert_add_fusion = (f32[256,2048]{1,0:T(8,128)}, f32[256]{0:T(256)S(1)}) fusion(bf16[256,2048]{1,0:T(8,128)(2,1)S(1)} %copy-done.2, bf16[256,2048]{1,0:T(8,128)(2,1)} %all-reduce.2.cloned.1.call-done), kind=kLoop, calls=%fused_computation.9 | loop fusion | flops 2096896 | bytes 4195328 | tf_op jit(solution)/shard_map/add | solution.py:145
  159.1 0.5 multiply_reduce_fusion
  159.6 3.5 %fusion.58 = f32[256,512]{1,0:T(8,128)} fusion(bf16[2048,512]{1,0:T(8,128)(2,1)} %all-gather.6.cloned.1.call-done, f32[256]{0:T(256)S(1)} %add_rsqrt_fusion.1, f32[256]{0:T(256)S(1)} %broadcast_multiply_fusion.1, bf16[256,2048]{1,0:T(8,128)(2,1)} %all-reduce.2.cloned.1.call-done, bf16[256,2048]{1,0:T(8,128)(2,1)S(1)} %copy-done.2), kind=kOutput, calls=%fused_computation.117 | convolution fusion | flops 540016640 | bytes 4720640 | tf_op jit(solution)/shard_map/dot_general | solution.py:148
  163.1 16.8 %all-gather.8.cloned.1.call-done = bf16[2048,512]{1,0:T(8,128)(2,1)} async-done(((bf16[128,512]{1,0:T(8,128)(2,1)}), bf16[2048,512]{1,0:T(8,128)(2,1)}) %all-gather.8.cloned.1.call-update) | async-done | bytes 2097168 | tf_op jit(solution)/shard_map/all_gather | solution.py:155
  179.9 5.1 %convolution_convert_fusion = bf16[256,2048]{1,0:T(8,128)(2,1)} fusion(bf16[512,2048]{1,0:T(8,128)(2,1)} %constant_dynamic-update-slice_fusion, bf16[2048,512]{1,0:T(8,128)(2,1)} %all-gather.8.cloned.1.call-done, f32[256,512]{1,0:T(8,128)} %fusion.58, f32[256]{0:T(256)S(1)} %add_rsqrt_fusion.1, f32[256]{0:T(256)S(1)} %broadcast_multiply_fusion.1, ...), kind=kOutput, calls=%fused_computation.12 | convolution fusion | flops 1078198272 | bytes 7866368 | tf_op jit(solution)/shard_map/dot_general | solution.py:194
  185.1 17.8 %all-to-all-done = bf16[16,1,256,512]{3,2,1,0:T(8,128)(2,1)} async-done(((bf16[16,1,256,512]{3,2,1,0:T(8,128)(2,1)}), bf16[16,1,256,512]{3,2,1,0:T(8,128)(2,1)}, u32[]{:S(2)}, u32[]{:S(2)}) %all-to-all-start) | async-done | bytes 4194336 | tf_op jit(solution)/shard_map/all_to_all | solution.py:129
  202.9 6.8 %convert_element_type.101 = f32[16,1,256,512]{3,2,1,0:T(8,128)} convert(bf16[16,1,256,512]{3,2,1,0:T(8,128)(2,1)} %all-to-all-done) | non-fusion elementwise | flops 2097152 | bytes 12582912 | tf_op jit(solution)/shard_map/convert_element_type | solution.py:135
  209.8 17.9 %reduce-scatter.2.cloned.1.call-done = bf16[32,2048]{1,0:T(8,128)(2,1)} async-done(((bf16[256,2048]{1,0:T(8,128)(2,1)}), bf16[32,2048]{1,0:T(8,128)(2,1)}) %reduce-scatter.2.cloned.1.call-update) | async-done | bytes 131088 | tf_op jit(solution)/shard_map/reduce_scatter | solution.py:197
  227.7 1.7 add_convert_fusion
  (65 shorter events, 0.9 us)
Async XLA Ops:
  8.0 47.6 %copy-start = (bf16[512,2048]{1,0:T(8,128)(2,1)S(1)}, bf16[512,2048]{1,0:T(8,128)(2,1)}, u32[]{:S(2)}) copy-start(bf16[512,2048]{1,0:T(8,128)(2,1)} %param.22) | copy-start | bytes 6291460
  8.0 28.6 %all-gather.4.cloned.1.call-start = ((), (), s32[]{:S(2)}) async-start(), calls=%async_computation.2 | async-start | bytes 1179648 | tf_op jit(solution)/shard_map/all_gather | solution.py:106
  8.7 147.3 %all-reduce.2.cloned.1.call-start = ((), (), s32[]{:S(2)}) async-start(), calls=%async_computation.3 | async-start | bytes 2097152 | tf_op jit(solution)/shard_map/psum | solution.py:144
  36.6 8.3 %copy-start.1 = (f32[16,1,256,512]{3,2,1,0:T(8,128)S(1)}, f32[16,1,256,512]{3,2,1,0:T(8,128)}, u32[]{:S(2)}) copy-start(f32[16,1,256,512]{3,2,1,0:T(8,128)} %param.14) | copy-start | bytes 25165828
  38.2 10.4 %copy-start.9 = (f32[256]{0:T(256)}, f32[256]{0:T(256)S(1)}, u32[]{:S(2)}) copy-start(f32[256]{0:T(256)S(1)} %broadcast_multiply_fusion.2) | copy-start | bytes 3076
  40.2 8.4 %copy-start.11 = (f32[256]{0:T(256)}, f32[256]{0:T(256)S(1)}, u32[]{:S(2)}) copy-start(f32[256]{0:T(256)S(1)} %add_rsqrt_fusion.2) | copy-start | bytes 3076
  44.9 3.7 %copy-start.5 = (bf16[16,16,128]{2,1,0:T(8,128)(2,1)}, bf16[16,16,128]{2,1,0:T(8,128)(2,1)S(1)}, u32[]{:S(2)}) copy-start(bf16[16,16,128]{2,1,0:T(8,128)(2,1)S(1)} %get-tuple-element.10) | copy-start | bytes 196612
  44.9 3.7 %copy-start.6 = (bf16[16,16,128]{2,1,0:T(8,128)(2,1)}, bf16[16,16,128]{2,1,0:T(8,128)(2,1)S(1)}, u32[]{:S(2)}) copy-start(bf16[16,16,128]{2,1,0:T(8,128)(2,1)S(1)} %get-tuple-element.11) | copy-start | bytes 196612
  45.0 3.7 %copy-start.2 = (bf16[256,2048]{1,0:T(8,128)(2,1)S(1)}, bf16[256,2048]{1,0:T(8,128)(2,1)}, u32[]{:S(2)}) copy-start(bf16[256,2048]{1,0:T(8,128)(2,1)} %all-gather.4.cloned.1.call-done) | copy-start | bytes 3145732
  45.0 3.7 %copy-start.12 = (bf16[2048,512]{1,0:T(8,128)(2,1)S(1)}, bf16[2048,512]{1,0:T(8,128)(2,1)}, u32[]{:S(2)}) copy-start(bf16[2048,512]{1,0:T(8,128)(2,1)} %param.20) | copy-start | bytes 6291460
  52.9 2.4 %copy-start.3 = (f32[16,16,1,512]{3,1,0,2:T(8,128)S(1)}, f32[16,16,1,512]{3,1,0,2:T(8,128)}, u32[]{:S(2)}) copy-start(f32[16,16,1,512]{3,1,0,2:T(8,128)} %get-tuple-element.15) | copy-start | bytes 1572868
  55.6 7.9 %copy-start.13 = (s32[16]{0:T(128)S(1)}, s32[16]{0:T(128)}, u32[]{:S(2)}) copy-start(s32[16]{0:T(128)} %param.17) | copy-start | bytes 196
  57.4 102.2 %all-gather.6.cloned.1.call-start = ((), (), s32[]{:S(2)}) async-start(), calls=%async_computation.4 | async-start | bytes 2228224 | tf_op jit(solution)/shard_map/all_gather | solution.py:150
  58.0 121.9 %all-gather.8.cloned.1.call-start = ((), (), s32[]{:S(2)}) async-start(), calls=%async_computation.5 | async-start | bytes 2228224 | tf_op jit(solution)/shard_map/all_gather | solution.py:155
  58.1 9.4 %collective-permute-start = (bf16[512,128]{1,0:T(8,128)(2,1)}, bf16[512,128]{1,0:T(8,128)(2,1)}, u32[]{:S(2)}, u32[]{:S(2)}) collective-permute-start(bf16[512,128]{1,0:T(8,128)(2,1)} %param.25), channel_id=1, source_target_pairs={{0,8},{8,16},{16,24},{24,32},{32,40},{40,48},{48,56},{56,64},{64,7... | collective-permute-start | bytes 393224 | tf_op jit(solution)/shard_map/ppermute | solution.py:177
  59.6 7.8 %collective-permute-start.1 = (bf16[512,128]{1,0:T(8,128)(2,1)}, bf16[512,128]{1,0:T(8,128)(2,1)}, u32[]{:S(2)}, u32[]{:S(2)}) collective-permute-start(bf16[512,128]{1,0:T(8,128)(2,1)} %param.25), channel_id=1, source_target_pairs={{0,120},{8,0},{16,8},{24,16},{32,24},{40,32},{48,40},{56,48},{64,5... | collective-permute-start | bytes 393224 | tf_op jit(solution)/shard_map/ppermute | solution.py:187
  64.0 1.6 copy-start.7
  65.6 66.8 %copy-start.8 = (f32[16,16]{1,0:T(8,128)S(1)}, f32[16,16]{1,0:T(8,128)}, u32[]{:S(2)}) copy-start(f32[16,16]{1,0:T(8,128)} %get-tuple-element.16) | copy-start | bytes 3076
  65.6 66.8 %copy-start.10 = (f32[16]{0:T(128)S(1)}, f32[16]{0:T(128)}, u32[]{:S(2)}) copy-start(f32[16]{0:T(128)} %get-tuple-element.13) | copy-start | bytes 196
  67.5 8.7 %collective-permute-start.2 = (bf16[512,128]{1,0:T(8,128)(2,1)}, bf16[512,128]{1,0:T(8,128)(2,1)S(1)}, u32[]{:S(2)}, u32[]{:S(2)}) collective-permute-start(bf16[512,128]{1,0:T(8,128)(2,1)} %collective-permute-done), channel_id=1, source_target_pairs={{0,8},{8,16},{16,24},{24,32},{32,40},{40,48},{48,56},{56,64},{64,7... | collective-permute-start | bytes 393224 | tf_op jit(solution)/shard_map/ppermute | solution.py:177
  67.5 8.7 %collective-permute-start.3 = (bf16[512,128]{1,0:T(8,128)(2,1)}, bf16[512,128]{1,0:T(8,128)(2,1)S(1)}, u32[]{:S(2)}, u32[]{:S(2)}) collective-permute-start(bf16[512,128]{1,0:T(8,128)(2,1)} %collective-permute-done.1), channel_id=1, source_target_pairs={{0,120},{8,0},{16,8},{24,16},{32,24},{40,32},{48,40},{56,48},{64,5... | collective-permute-start | bytes 393224 | tf_op jit(solution)/shard_map/ppermute | solution.py:187
  76.1 8.6 %collective-permute-start.4 = (bf16[512,128]{1,0:T(8,128)(2,1)S(1)}, bf16[512,128]{1,0:T(8,128)(2,1)S(1)}, u32[]{:S(2)}, u32[]{:S(2)}) collective-permute-start(bf16[512,128]{1,0:T(8,128)(2,1)S(1)} %collective-permute-done.2), channel_id=1, source_target_pairs={{0,8},{8,16},{16,24},{24,32},{32,40},{40,48},{48,56},{56,64},{64,7... | collective-permute-start | bytes 393224 | tf_op jit(solution)/shard_map/ppermute | solution.py:177
  76.1 8.6 %collective-permute-start.5 = (bf16[512,128]{1,0:T(8,128)(2,1)S(1)}, bf16[512,128]{1,0:T(8,128)(2,1)S(1)}, u32[]{:S(2)}, u32[]{:S(2)}) collective-permute-start(bf16[512,128]{1,0:T(8,128)(2,1)S(1)} %collective-permute-done.3), channel_id=1, source_target_pairs={{0,120},{8,0},{16,8},{24,16},{32,24},{40,32},{48,40},{56,48},{64,5... | collective-permute-start | bytes 393224 | tf_op jit(solution)/shard_map/ppermute | solution.py:187
  84.8 8.3 %collective-permute-start.6 = (bf16[512,128]{1,0:T(8,128)(2,1)S(1)}, bf16[512,128]{1,0:T(8,128)(2,1)S(1)}, u32[]{:S(2)}, u32[]{:S(2)}) collective-permute-start(bf16[512,128]{1,0:T(8,128)(2,1)S(1)} %collective-permute-done.4), channel_id=1, source_target_pairs={{0,8},{8,16},{16,24},{24,32},{32,40},{40,48},{48,56},{56,64},{64,7... | collective-permute-start | bytes 393224 | tf_op jit(solution)/shard_map/ppermute | solution.py:177
  84.8 10.3 %collective-permute-start.7 = (bf16[512,128]{1,0:T(8,128)(2,1)S(1)}, bf16[512,128]{1,0:T(8,128)(2,1)S(1)}, u32[]{:S(2)}, u32[]{:S(2)}) collective-permute-start(bf16[512,128]{1,0:T(8,128)(2,1)S(1)} %collective-permute-done.5), channel_id=1, source_target_pairs={{0,120},{8,0},{16,8},{24,16},{32,24},{40,32},{48,40},{56,48},{64,5... | collective-permute-start | bytes 393224 | tf_op jit(solution)/shard_map/ppermute | solution.py:187
  93.1 9.4 %collective-permute-start.8 = (bf16[512,128]{1,0:T(8,128)(2,1)S(1)}, bf16[512,128]{1,0:T(8,128)(2,1)S(1)}, u32[]{:S(2)}, u32[]{:S(2)}) collective-permute-start(bf16[512,128]{1,0:T(8,128)(2,1)S(1)} %collective-permute-done.6), channel_id=1, source_target_pairs={{0,8},{8,16},{16,24},{24,32},{32,40},{40,48},{48,56},{56,64},{64,7... | collective-permute-start | bytes 393224 | tf_op jit(solution)/shard_map/ppermute | solution.py:177
  95.1 11.4 %collective-permute-start.9 = (bf16[512,128]{1,0:T(8,128)(2,1)S(1)}, bf16[512,128]{1,0:T(8,128)(2,1)S(1)}, u32[]{:S(2)}, u32[]{:S(2)}) collective-permute-start(bf16[512,128]{1,0:T(8,128)(2,1)S(1)} %collective-permute-done.7), channel_id=1, source_target_pairs={{0,120},{8,0},{16,8},{24,16},{32,24},{40,32},{48,40},{56,48},{64,5... | collective-permute-start | bytes 393224 | tf_op jit(solution)/shard_map/ppermute | solution.py:187
  102.4 11.2 %collective-permute-start.10 = (bf16[512,128]{1,0:T(8,128)(2,1)S(1)}, bf16[512,128]{1,0:T(8,128)(2,1)S(1)}, u32[]{:S(2)}, u32[]{:S(2)}) collective-permute-start(bf16[512,128]{1,0:T(8,128)(2,1)S(1)} %collective-permute-done.8), channel_id=1, source_target_pairs={{0,8},{8,16},{16,24},{24,32},{32,40},{40,48},{48,56},{56,64},{64,7... | collective-permute-start | bytes 393224 | tf_op jit(solution)/shard_map/ppermute | solution.py:177
  106.5 9.3 %collective-permute-start.11 = (bf16[512,128]{1,0:T(8,128)(2,1)S(1)}, bf16[512,128]{1,0:T(8,128)(2,1)S(1)}, u32[]{:S(2)}, u32[]{:S(2)}) collective-permute-start(bf16[512,128]{1,0:T(8,128)(2,1)S(1)} %collective-permute-done.9), channel_id=1, source_target_pairs={{0,120},{8,0},{16,8},{24,16},{32,24},{40,32},{48,40},{56,48},{64,5... | collective-permute-start | bytes 393224 | tf_op jit(solution)/shard_map/ppermute | solution.py:187
  113.6 9.3 %collective-permute-start.12 = (bf16[512,128]{1,0:T(8,128)(2,1)S(1)}, bf16[512,128]{1,0:T(8,128)(2,1)S(1)}, u32[]{:S(2)}, u32[]{:S(2)}) collective-permute-start(bf16[512,128]{1,0:T(8,128)(2,1)S(1)} %collective-permute-done.10), channel_id=1, source_target_pairs={{0,8},{8,16},{16,24},{24,32},{32,40},{40,48},{48,56},{56,64},{64,7... | collective-permute-start | bytes 393224 | tf_op jit(solution)/shard_map/ppermute | solution.py:177
  115.8 8.3 %collective-permute-start.13 = (bf16[512,128]{1,0:T(8,128)(2,1)S(1)}, bf16[512,128]{1,0:T(8,128)(2,1)S(1)}, u32[]{:S(2)}, u32[]{:S(2)}) collective-permute-start(bf16[512,128]{1,0:T(8,128)(2,1)S(1)} %collective-permute-done.11), channel_id=1, source_target_pairs={{0,120},{8,0},{16,8},{24,16},{32,24},{40,32},{48,40},{56,48},{64,5... | collective-permute-start | bytes 393224 | tf_op jit(solution)/shard_map/ppermute | solution.py:187
  122.9 8.8 %collective-permute-start.14 = (bf16[512,128]{1,0:T(8,128)(2,1)S(1)}, bf16[512,128]{1,0:T(8,128)(2,1)S(1)}, u32[]{:S(2)}, u32[]{:S(2)}) collective-permute-start(bf16[512,128]{1,0:T(8,128)(2,1)S(1)} %collective-permute-done.12), channel_id=1, source_target_pairs={{0,8},{8,16},{16,24},{24,32},{32,40},{40,48},{48,56},{56,64},{64,7... | collective-permute-start | bytes 393224 | tf_op jit(solution)/shard_map/ppermute | solution.py:177
  151.4 51.5 %all-to-all-start = ((bf16[16,1,256,512]{3,2,1,0:T(8,128)(2,1)}), bf16[16,1,256,512]{3,2,1,0:T(8,128)(2,1)}, u32[]{:S(2)}, u32[]{:S(2)}) async-start(bf16[16,1,256,512]{3,2,1,0:T(8,128)(2,1)} %fusion.4), calls=%async_computation.1 | async-start | bytes 8388608 | tf_op jit(solution)/shard_map/all_to_all | solution.py:129
  156.0 71.7 %reduce-scatter.2.cloned.1.call-start = ((), (), s32[]{:S(2)}) async-start(), calls=%async_computation.6 | async-start | bytes 1179648 | tf_op jit(solution)/shard_map/reduce_scatter | solution.py:197
  156.1 3.0 %copy-start.4 = (bf16[256,2048]{1,0:T(8,128)(2,1)S(1)}, bf16[256,2048]{1,0:T(8,128)(2,1)}, u32[]{:S(2)}) copy-start(bf16[256,2048]{1,0:T(8,128)(2,1)} %all-reduce.2.cloned.1.call-done) | copy-start | bytes 3145732
Sparse Core Ops, SparseCore 0:
  10.6 26.0 all-gather.3
  57.6 63.3 all-reduce.1
  185.2 42.4 reduce-scatter.1
Sparse Core Ops, SparseCore 1:
  60.1 48.3 all-gather.5
  110.4 69.5 all-gather.7
